TPU v7x, 32 devices: a whole 2x2x4 slice. The times are simulated.
32 devices in a mesh: child: 2 (over x), row: 4 (over z), col: 4 (over y, core).
Axes of the slice: x: 2, y: 2, z: 4, core: 2. Of those that a mesh axis runs over, the one named last changes fastest.
Arguments:
- contrib: float32 [2, 2048, 2048], P('child', 'row', 'col'), may hold values from -0.125 to 0.125
- assembled: float32 [2, 2048, 4096], P('child', 'row', 'col'), may hold values from -0.125 to 0.125
- pattern: int32 [16, 16], P('row', 'col'), may hold values 0 or 1
- omega: float32 [4096, 256], P('col', 'row'), may hold values from -6 to 6
- row_maps: int32 [2, 2048], P('child'), may hold values from 0 to 4095, as said below
- leaf_bounds: int32 [4], P('row'), may hold values from 448 to 576
Outputs:
- bases: float32 [4096, 256], P('row', ('child', 'col'))
- coupling: float32 [4, 2, 256, 256], P('row', None, ('child', 'col'))
Inputs may be any that keep to these rules, and one draw needn't show every extreme that they name: `row_maps`: for each child, entries k * 512 to (k + 1) * 512 - 1 are distinct, rising, and lie in k * 1024 to (k + 1) * 1024 - 1.
All inputs are finite; a program needn't handle non-finite values. No bound on the sum of `pattern` on one device may be relied on, other than what follows from the above.
Results may differ from a plain program's by a relative error of at most 0.0003.
Values sent between devices are 32-bit elements; how exact they have to be, the bound alone decides.
A program may use at most 64 MiB of HBM per device.

v0:
```python
import jax
import jax.numpy as jnp
from jax import lax
from jax.sharding import PartitionSpec as P

R = 256
BT = 256


highest = lax.Precision.HIGHEST


def partner(block, axis, distance):
    count = lax.axis_size(axis)
    route = []
    for low in range(count):
        high = low | 1 << distance
        if high != low and high < count:
            route += [(low, high), (high, low)]
    return lax.ppermute(block, axis, route)


def window_leaves(window, leaf_bound, counts):
    window_rows = window.shape[0]
    upper = window_rows // 2 + window_rows // 16
    lower = window_rows // 2 - window_rows // 16
    positions = jnp.arange(window_rows, dtype=jnp.int32)
    first_leaf = (positions < leaf_bound)[:, None]
    head_rows = window[:upper]
    tail_rows = window[lower:]
    head_masked = jnp.where(first_leaf[:upper], head_rows, 0.0)
    tail_masked = jnp.where(first_leaf[lower:], 0.0, tail_rows)
    head_gram = jnp.dot(head_masked.T, head_rows, precision=highest)
    tail_gram = jnp.dot(tail_masked.T, tail_rows, precision=highest)
    factors = jnp.linalg.cholesky(jnp.stack([head_gram, tail_gram]) / counts)
    head_part = lax.linalg.triangular_solve(
        factors[0], head_rows, left_side=False, lower=True, transpose_a=True
    )
    tail_part = lax.linalg.triangular_solve(
        factors[1], tail_rows, left_side=False, lower=True, transpose_a=True
    )
    middle = jnp.where(first_leaf[lower:upper], head_part[lower:], tail_part[: upper - lower])
    whole = jnp.concatenate([head_part[:lower], middle, tail_part[upper - lower :]], axis=0)
    return (factors, whole)


def local(contrib, assembled, pattern, omega, row_maps, leaf_bounds):
    tile_rows = contrib.shape[1]
    tile_cols = contrib.shape[2]
    window_rows = omega.shape[0]
    slice_width = R // (2 * lax.axis_size("col"))
    row_pos = lax.axis_index("row")
    col_pos = lax.axis_index("col")
    half_pos = lax.axis_index("child")
    group_pos = half_pos * lax.axis_size("col") + col_pos
    zero_index = jnp.zeros((), jnp.int32)
    child_maps = row_maps[0]
    column_maps = (
        lax.dynamic_slice_in_dim(child_maps, col_pos * tile_cols, tile_cols) - col_pos * window_rows
    )
    target_maps = (
        lax.dynamic_slice_in_dim(child_maps, row_pos * tile_rows, tile_rows) - row_pos * window_rows
    )
    full_omega = lax.all_gather(omega, "row", axis=1, tiled=True)
    picked = jnp.take(full_omega, column_maps, axis=0)
    product = jnp.dot(contrib[0], picked, precision=highest)
    pattern_rows = lax.dynamic_slice_in_dim(
        pattern, half_pos * (tile_rows // BT), tile_rows // BT, 0
    ).astype(jnp.float32)
    masked = (
        assembled[0].reshape(tile_rows // BT, BT, window_rows // BT, BT)
        * pattern_rows[:, None, :, None]
    ).reshape(tile_rows, window_rows)
    sparse = jnp.dot(masked, full_omega, precision=highest)
    spread = jnp.zeros((window_rows, R), jnp.float32).at[target_maps].add(product)
    placed = lax.dynamic_update_slice(
        jnp.zeros((window_rows, R), jnp.float32), sparse, (half_pos * tile_rows, zero_index)
    )
    samples = lax.psum_scatter(spread + placed, ("child", "col"), scatter_dimension=1, tiled=True)
    leaf_bound = leaf_bounds[0]
    head_count = leaf_bound.astype(jnp.float32)
    tail_count = (window_rows - leaf_bound).astype(jnp.float32)
    counts = jnp.stack([head_count, tail_count])[:, None, None]
    window = lax.all_gather(samples, ("child", "col"), axis=1, tiled=True)
    factors, whole = window_leaves(window, leaf_bound, counts)
    bases = lax.dynamic_slice_in_dim(whole, group_pos * slice_width, slice_width, 1)
    own_cols = lax.dynamic_slice_in_dim(factors, group_pos * slice_width, slice_width, 2)
    sibling = partner(factors, "row", 0)
    coupling = jnp.einsum("lab,lac->lbc", own_cols, sibling, precision=highest)
    return (bases, coupling[None])


def solution(mesh):
    in_specs = (
        P("child", "row", "col"),
        P("child", "row", "col"),
        P("row", "col"),
        P("col", "row"),
        P("child", None),
        P("row"),
    )
    out_specs = (P("row", ("child", "col")), P("row", None, ("child", "col"), None))
    return jax.shard_map(local, mesh=mesh, in_specs=in_specs, out_specs=out_specs, check_vma=False)
```

profile of v0, /device:TPU:0, one launch (start us, length us, event | category | flops | bytes accessed | tf_op | source)
XLA Modules:
  0.0 277.7 jit_solution(4104742253993452384)
XLA Ops:
  9.0 1.8 copy.75
  10.9 29.4 %all-gather.3.cloned.1.call-done = f32[1024,256]{0,1:T(8,128)} async-done(((f32[1024,64]{0,1:T(8,128)}), f32[1024,256]{0,1:T(8,128)}) %all-gather.3.cloned.1.call-update) | async-done | bytes 1048592 | tf_op jit(solution)/shard_map/all_gather | solution.py:64
  40.3 1.6 copy.47
  41.9 2.2 gather_fusion
  44.1 3.9 %convolution_bitcast_fusion = f32[512,256]{0,1:T(8,128)} fusion(f32[1,512,512]{2,1,0:T(8,128)S(1)} %copy-done, f32[512,256]{1,0:T(8,128)} %gather_fusion, pred[512]{0:T(512)(128)(4,1)S(1)} %compare_and_fusion), kind=kOutput, calls=%fused_computation.8 | convolution fusion | flops 805437440 | bytes 2097664 | tf_op jit(solution)/shard_map/dot_general | solution.py:66
  48.0 2.1 copy.48
  50.1 4.8 %scatter_custom_fusion = f32[1024,256]{1,0:T(8,128)} fusion(s32[512]{0:T(512)S(1)} %bitcast.111, f32[512,256]{1,0:T(8,128)} %copy.48, f32[]{:T(128)} %constant.113.clone.1), kind=kCustom, calls=%fused_computation.37 | custom fusion | flops 131072 | bytes 1049088 | tf_op jit(solution)/shard_map/scatter-add | solution.py:75
  54.9 4.6 %fusion.2 = f32[1024,256]{1,0:T(8,128)} fusion(f32[1024,256]{1,0:T(8,128)} %scatter_custom_fusion, s32[]{:T(128)S(6)} %select_n.68, f32[1024,256]{0,1:T(8,128)} %all-gather.3.cloned.1.call-done, f32[512,1024]{1,0:T(8,128)S(1)} %bitcast.101, f32[1,512,1024]{2,1,0:T(8,128)} %param.9), kind=kOutput, calls=%fused_computation.10 | convolution fusion | flops 1611268096 | bytes 6291460 | tf_op jit(solution)/shard_map/dot_general | solution.py:74
  59.5 2.5 copy.67
  62.1 35.5 %reduce-scatter.4.cloned.1.call-done = f32[32,1024]{1,0:T(8,128)} async-done(((f32[256,1024]{1,0:T(8,128)}), f32[32,1024]{1,0:T(8,128)}) %reduce-scatter.4.cloned.1.call-update) | async-done | bytes 131088
  98.6 24.3 %all-gather.5.cloned.1.call-done = f32[1024,256]{0,1:T(8,128)} async-done(((f32[1024,32]{0,1:T(8,128)}), f32[1024,256]{0,1:T(8,128)}) %all-gather.5.cloned.1.call-update) | async-done | bytes 1048592 | tf_op jit(solution)/shard_map/all_gather | solution.py:84
  122.9 1.6 fusion.50
  125.8 2.0 convolution_bitcast_fusion.2
  131.8 23.6 %custom-call.16 = f32[2,128,128]{2,1,0:T(8,128)S(1)} custom-call(f32[2,128,128]{2,1,0:T(8,128)S(1)} %cholesky.122), custom_call_target="Cholesky" | custom-call | tf_op jit(solution)/shard_map/jit(cholesky)/cholesky | solution.py:35
  155.5 19.7 %custom-call.17 = f32[2,1,128,128]{2,3,1,0:T(8,128)S(1)} custom-call(f32[2,1,128,128]{3,2,1,0:T(8,128)S(1)} %select_bitcast_fusion), custom_call_target="InvertDiagBlocksLowerTriangular" | custom-call | tf_op jit(solution)/shard_map/jit(cholesky)/cholesky | solution.py:35
  177.7 23.5 %custom-call.18 = f32[2,128,128]{2,1,0:T(8,128)S(1)} custom-call(f32[2,128,128]{2,1,0:T(8,128)S(1)} %convolution_subtract_fusion.2), custom_call_target="Cholesky" | custom-call | tf_op jit(solution)/shard_map/jit(cholesky)/cholesky | solution.py:35
  201.5 1.6 collective-permute-start
  203.2 4.0 %while.5 = (s32[]{:T(128)}, f32[256,256]{1,0:T(8,128)S(1)}, s32[2,2]{1,0:T(2,128)S(1)}, f32[2,128,128]{2,1,0:T(8,128)S(1)}, s32[]{:T(128)}) while((s32[]{:T(128)}, f32[256,256]{1,0:T(8,128)S(1)}, s32[2,2]{1,0:T(2,128)S(1)}, f32[2,128,128]{2,1,0:T(8,128)S(1)}, s32[]{:T(128)}) %tuple.56), condition=%wide.while_cond.clone, body=%wide.while_body.clone.sunk | while | flops 2 | bytes 131181 | solution.py:39
  203.8 1.4 bitcast_dynamic-update-slice_fusion.5
  205.8 1.4 bitcast_dynamic-update-slice_fusion.5
  207.2 20.5 %custom-call.21 = f32[2,128,128]{1,2,0:T(8,128)} custom-call(f32[2,128,128]{2,1,0:T(8,128)S(1)} %get-tuple-element.18), custom_call_target="InvertDiagBlocksLowerTriangular" | custom-call | tf_op jit(solution)/shard_map/triangular_solve/custom-call.0 | solution.py:39
  228.7 1.9 copy.74
  230.5 1.6 fusion.16
  232.1 1.4 convolution_subtract_fusion
  235.4 5.1 %while.4 = (s32[]{:T(128)}, f32[256,256]{1,0:T(8,128)S(1)}, s32[2,2]{1,0:T(2,128)S(1)}, f32[2,128,128]{2,1,0:T(8,128)}, s32[]{:T(128)}) while((s32[]{:T(128)}, f32[256,256]{1,0:T(8,128)S(1)}, s32[2,2]{1,0:T(2,128)S(1)}, f32[2,128,128]{2,1,0:T(8,128)}, s32[]{:T(128)}) %tuple.65), condition=%wide.while_cond, body=%wide.while_body.sunk | while | flops 2 | bytes 132705 | solution.py:36
  236.0 2.0 bitcast_dynamic-update-slice_fusion.4
  238.6 2.0 bitcast_dynamic-update-slice_fusion.4
  240.6 21.1 %custom-call.20 = f32[2,128,128]{1,2,0:T(8,128)} custom-call(f32[2,128,128]{2,1,0:T(8,128)} %get-tuple-element.17), custom_call_target="InvertDiagBlocksLowerTriangular" | custom-call | tf_op jit(solution)/shard_map/triangular_solve/custom-call.0 | solution.py:36
  261.6 1.9 copy.72
  263.5 1.5 fusion.18
  265.0 1.4 convolution_subtract_fusion.1
  268.9 2.3 convolution_bitcast_fusion.3
  (64 shorter events, 18.2 us)
Async XLA Ops:
  7.2 36.9 %copy-start = (f32[1,512,512]{2,1,0:T(8,128)S(1)}, f32[1,512,512]{2,1,0:T(8,128)}, u32[]{:S(2)}) copy-start(f32[1,512,512]{2,1,0:T(8,128)} %param.8) | copy-start | bytes 3145732
  7.2 33.1 %all-gather.3.cloned.1.call-start = ((), (), s32[]{:S(2)}) async-start(), calls=%async_computation.1 | async-start | bytes 1310720 | tf_op jit(solution)/shard_map/all_gather | solution.py:64
  7.9 89.7 %reduce-scatter.4.cloned.1.call-start = ((), (), s32[]{:S(2)}) async-start(), calls=%async_computation.3 | async-start | bytes 1179648
  9.0 1.8 copy-start.4
  44.1 10.8 %copy-start.2 = (f32[64,8,4,256]{3,1,2,0:T(8,128)S(1)}, f32[64,8,4,256]{3,1,2,0:T(8,128)}, u32[]{:S(2)}) copy-start(f32[64,8,4,256]{3,1,2,0:T(8,128)} %copy.75) | copy-start | bytes 6291460
  62.1 60.8 %all-gather.5.cloned.1.call-start = ((), (), s32[]{:S(2)}) async-start(), calls=%async_computation.2 | async-start | bytes 1179648 | tf_op jit(solution)/shard_map/all_gather | solution.py:84
  122.9 2.9 %copy-start.1 = (f32[1024,256]{0,1:T(8,128)S(1)}, f32[1024,256]{0,1:T(8,128)}, u32[]{:S(2)}) copy-start(f32[1024,256]{0,1:T(8,128)} %all-gather.5.cloned.1.call-done) | copy-start | bytes 3145732
  131.0 0.8 copy-start.3
  201.5 67.3 %collective-permute-start = (f32[2,256,256]{2,1,0:T(8,128)S(1)}, f32[2,256,256]{2,1,0:T(8,128)}, u32[]{:S(2)}, u32[]{:S(2)}) collective-permute-start(f32[2,256,256]{2,1,0:T(8,128)S(1)} %select_select_fusion), channel_id=1, source_target_pairs={{0,4},{4,0},{8,12},{12,8},{1,5},{5,1},{9,13},{13,9},{2,6},{6,2},{1... | collective-permute-start | bytes 1572872 | tf_op jit(solution)/shard_map/ppermute | solution.py:20
Sparse Core Ops, SparseCore 0:
  9.6 30.6 all-gather.2
  62.2 35.3 reduce-scatter.3
  99.5 23.3 all-gather.4
where the time goes:
time: 279 us; the launch traced here: 278 us
  other arithmetic  116 us (42%)
  waiting for transfers between devices  89.9 us (32%)
  local copies, waits for them, and re-layouts  30.9 us (11%)
  matrix products  24.6 us (9%)
  between operations  14.7 us (5%)
    another operation x9, other arithmetic, window_leaves(): factors = jnp.linalg.cholesky(jnp.stack([head_gram, tail_gram]) / counts)  67 us
    unnamed x4, waiting for transfers between devices  36.2 us
    all_gather x1, waiting for transfers between devices, local(): full_omega = lax.all_gather(omega, 'row', axis=1, tiled=True)  29.4 us
    all_gather x1, waiting for transfers between devices, local(): window = lax.all_gather(samples, ('child', 'col'), axis=1, tiled=True)  24.3 us
    another operation x4, other arithmetic, window_leaves(): lax.linalg.triangular_solve(factors[0], head_rows, left_side=False, lower...  21.2 us
    another operation x2, other arithmetic, window_leaves(): lax.linalg.triangular_solve(factors[1], tail_rows, left_side=False, lower...  20.6 us
    unnamed x18, local copies, waits for them, and re-layouts  12.6 us
  transfers between devices with their start and end apart: 4, of which 3 were waited for; matrix products, arithmetic and copies ran while one was open for 25% of the time, Pallas kernels for 0%

commit v1 on v0

v1 whole, which is shorter than its diff:
```python
import functools

import jax
import jax.numpy as jnp
from jax import lax
from jax.experimental import pallas as pl
from jax.experimental.pallas import tpu as pltpu
from jax.sharding import PartitionSpec as P

BT = 256
NB = 64
SUB = 8
MESH = pl.DeviceIdType.MESH
highest = lax.Precision.HIGHEST
VMEM = pl.BlockSpec(memory_space=pltpu.VMEM)
SMEM = pl.BlockSpec(memory_space=pltpu.SMEM)

NN = (((1,), (0,)), ((), ()))
NT = (((1,), (1,)), ((), ()))
TN = (((0,), (0,)), ((), ()))


def mm(a, b, dims=NN):
    return lax.dot_general(a, b, dims, precision=highest, preferred_element_type=jnp.float32)


def split(a):
    high = a.astype(jnp.bfloat16)
    low = (a - high.astype(jnp.float32)).astype(jnp.bfloat16)
    return high, low


def dot16(a, b, dims=NN):
    return lax.dot_general(a, b, dims, preferred_element_type=jnp.float32)


def mm3(a, b, dims=NN):
    (ah, al), (bh, bl) = split(a), split(b)
    return dot16(ah, bh, dims) + (dot16(ah, bl, dims) + dot16(al, bh, dims))


def gather_kernel(own_ref, out_ref, send_right, send_left, recv, local_sem):
    count = lax.axis_size("row")
    me = lax.axis_index("row")
    has_left = me > 0
    has_right = me < count - 1
    barrier = pltpu.get_barrier_semaphore()

    @pl.when(has_left)
    def _():
        pl.semaphore_signal(barrier, inc=1, device_id={"row": me - 1}, device_id_type=MESH)

    @pl.when(has_right)
    def _():
        pl.semaphore_signal(barrier, inc=1, device_id={"row": me + 1}, device_id_type=MESH)

    keep = pltpu.make_async_copy(own_ref, out_ref.at[me], local_sem)
    keep.start()

    pl.semaphore_wait(barrier, jnp.minimum(me, 1) + jnp.minimum(count - 1 - me, 1))

    def hop(block, source, target, sems):
        return pltpu.make_async_remote_copy(
            src_ref=source,
            dst_ref=out_ref.at[block],
            send_sem=sems.at[block],
            recv_sem=recv.at[block],
            device_id={"row": target},
            device_id_type=MESH,
        )

    for step in range(count):
        low = me - step
        high = me + step
        from_left = low >= 0
        from_right = high < count
        source_low = own_ref if step == 0 else out_ref.at[low]
        source_high = own_ref if step == 0 else out_ref.at[high]
        if step > 0:

            @pl.when(from_left)
            def _():
                hop(low, source_low, me - 1, send_right).wait_recv()

        @pl.when(jnp.logical_and(from_left, has_right))
        def _():
            hop(low, source_low, me + 1, send_right).start()

        if step > 0:

            @pl.when(from_right)
            def _():
                hop(high, source_high, me + 1, send_left).wait_recv()

        @pl.when(jnp.logical_and(from_right, has_left))
        def _():
            hop(high, source_high, me - 1, send_left).start()

    for step in range(count):
        low = me - step
        high = me + step
        source_low = own_ref if step == 0 else out_ref.at[low]
        source_high = own_ref if step == 0 else out_ref.at[high]

        @pl.when(jnp.logical_and(low >= 0, has_right))
        def _():
            hop(low, source_low, me + 1, send_right).wait_send()

        @pl.when(jnp.logical_and(high < count, has_left))
        def _():
            hop(high, source_high, me - 1, send_left).wait_send()

    keep.wait()


def gather_rows(own):
    count = lax.axis_size("row")
    return pl.pallas_call(
        gather_kernel,
        out_shape=jax.ShapeDtypeStruct((count,) + own.shape, jnp.float32),
        in_specs=[VMEM],
        out_specs=VMEM,
        scratch_shapes=[
            pltpu.SemaphoreType.DMA((count,)),
            pltpu.SemaphoreType.DMA((count,)),
            pltpu.SemaphoreType.DMA((count,)),
            pltpu.SemaphoreType.DMA,
        ],
        compiler_params=pltpu.CompilerParams(collective_id=0, has_side_effects=True),
        name="gather_rows",
    )(own)


def sketch_kernel(pattern_ref, omega_ref, contrib_ref, assembled_ref, columns_ref, targets_ref, out_ref):
    half = lax.axis_index("child")
    tile_rows, tile_cols = contrib_ref.shape
    window_rows = omega_ref.shape[1]
    omega_high, omega_low = split(omega_ref[...])
    lanes = lax.broadcasted_iota(jnp.int32, (window_rows, tile_cols), 0)
    pick = jnp.where(lanes == columns_ref[...], 1.0, 0.0).astype(jnp.bfloat16)
    picked_high = dot16(omega_high, pick).astype(jnp.bfloat16)
    picked_low = dot16(omega_low, pick).astype(jnp.bfloat16)
    front_high, front_low = split(contrib_ref[...])
    product = dot16(picked_high, front_high, NT) + (
        dot16(picked_high, front_low, NT) + dot16(picked_low, front_high, NT)
    )
    product_high, product_low = split(product)
    rows = lax.broadcasted_iota(jnp.int32, (tile_rows, window_rows), 1)
    place = jnp.where(rows == targets_ref[...], 1.0, 0.0).astype(jnp.bfloat16)
    out_ref[...] = dot16(product_high, place) + dot16(product_low, place)
    for row in range(tile_rows // BT):
        blocks = []
        for col in range(window_rows // BT):
            tile = assembled_ref[row * BT : (row + 1) * BT, col * BT : (col + 1) * BT]
            blocks.append(tile * pattern_ref[half * (tile_rows // BT) + row, col].astype(jnp.float32))
        masked_high, masked_low = split(jnp.concatenate(blocks, axis=1))
        sparse = dot16(omega_high, masked_high, NT) + (
            dot16(omega_high, masked_low, NT) + dot16(omega_low, masked_high, NT)
        )
        where = pl.ds(pl.multiple_of(half * tile_rows + row * BT, BT), BT)
        out_ref[:, where] = out_ref[:, where] + sparse


def sketch(pattern, omega, contrib, assembled, columns, targets):
    return pl.pallas_call(
        sketch_kernel,
        out_shape=jax.ShapeDtypeStruct(omega.shape, jnp.float32),
        in_specs=[SMEM, VMEM, VMEM, VMEM, VMEM, VMEM],
        out_specs=VMEM,
        compiler_params=pltpu.CompilerParams(vmem_limit_bytes=48 << 20),
        name="sketch",
    )(pattern, omega, contrib, assembled, columns, targets)


def reduce_kernel(part_ref, out_ref, pair_buf, sum_buf, chip_buf, *sems):
    pair_send, pair_recv, chip_send, chip_recv, all_send, all_recv, last_send, last_recv = sems
    col_count = lax.axis_size("col")
    chips = part_ref.shape[0]
    col = lax.axis_index("col")
    group = lax.axis_index("child") * col_count + col
    chip = group // 2
    core = group % 2
    other = 1 - core

    def device(chip_index, core_index):
        flat = chip_index * 2 + core_index
        return {"child": flat // col_count, "col": flat % col_count}

    def copy(source, target, send, recv, index, device_id, recv_index):
        return pltpu.make_async_remote_copy(
            src_ref=source,
            dst_ref=target,
            send_sem=send.at[index],
            recv_sem=recv.at[recv_index],
            device_id=device_id,
            device_id_type=MESH,
        )

    order = [lax.rem(chip + step, chips) for step in range(chips)]
    partner = device(chip, other)
    barrier = pltpu.get_barrier_semaphore()
    pl.semaphore_signal(barrier, inc=1, device_id=partner, device_id_type=MESH)
    for step in range(1, chips):
        pl.semaphore_signal(barrier, inc=1, device_id=device(order[step], core), device_id_type=MESH)
    pl.semaphore_wait(barrier, chips)

    steps = list(range(1, chips)) + [0]
    pair = {}
    for step in steps:
        c = order[step]
        pair[step] = copy(part_ref.at[c, other], pair_buf.at[c], pair_send, pair_recv, c, partner, c)
        pair[step].start()
    sends = {}
    for step in range(1, chips):
        c = order[step]
        pair[step].wait_recv()
        sum_buf[c] = part_ref[c, core] + pair_buf[c]
        sends[step] = copy(sum_buf.at[c], chip_buf.at[chip], chip_send, chip_recv, c, device(c, core), chip)
        sends[step].start()
    pair[0].wait_recv()
    total = part_ref[chip, core] + pair_buf[chip]
    for step in range(1, chips):
        c = order[step]
        copy(sum_buf.at[c], chip_buf.at[c], chip_send, chip_recv, c, device(c, core), c).wait_recv()
        total = total + chip_buf[c]
    out_ref[chip, core] = total
    spread = {}
    for step in range(1, chips):
        c = order[step]
        spread[step] = copy(
            out_ref.at[chip, core], out_ref.at[chip, core], all_send, all_recv, c, device(c, core), chip
        )
        spread[step].start()
    last = {}
    last[0] = copy(out_ref.at[chip, core], out_ref.at[chip, core], last_send, last_recv, chip, partner, chip)
    last[0].start()
    for step in range(1, chips):
        c = order[step]
        copy(out_ref.at[c, core], out_ref.at[c, core], all_send, all_recv, c, device(c, core), c).wait_recv()
        last[step] = copy(out_ref.at[c, core], out_ref.at[c, core], last_send, last_recv, c, partner, c)
        last[step].start()
    for step in range(chips):
        c = order[step]
        copy(out_ref.at[c, other], out_ref.at[c, other], last_send, last_recv, c, partner, c).wait_recv()
    for step in range(chips):
        pair[step].wait_send()
        last[step].wait_send()
    for step in range(1, chips):
        sends[step].wait_send()
        spread[step].wait_send()


def reduce_windows(part):
    chips = lax.axis_size("col") * lax.axis_size("child") // 2
    columns, window_rows = part.shape
    width = columns // (2 * chips)
    part = part.reshape(chips, 2, width, window_rows)
    block = pltpu.VMEM((chips, width, window_rows), jnp.float32)
    out = pl.pallas_call(
        reduce_kernel,
        out_shape=jax.ShapeDtypeStruct(part.shape, jnp.float32),
        in_specs=[VMEM],
        out_specs=VMEM,
        scratch_shapes=[block, block, block] + [pltpu.SemaphoreType.DMA((chips,))] * 8,
        compiler_params=pltpu.CompilerParams(collective_id=1, has_side_effects=True),
        name="reduce_windows",
    )(part)
    return out.reshape(columns, window_rows)


def eliminate(leaves):
    groups = NB // SUB
    index = lax.broadcasted_iota(jnp.int32, (SUB, 2 * NB), 0)
    wide = (SUB, 2 * NB)
    leaves = [list(rows) for rows in leaves]
    for panel in range(groups):
        first = panel * SUB
        columns = [
            {
                q: [jnp.broadcast_to(rows[q][:, first + k : first + k + 1], wide) for k in range(SUB)]
                for q in range(panel, groups)
            }
            for rows in leaves
        ]
        for k in range(SUB):
            for rows, cols in zip(leaves, columns):
                own = cols[panel]
                scale = lax.rsqrt(jnp.broadcast_to(own[k][k : k + 1], wide))
                pivot = jnp.broadcast_to(rows[panel][k : k + 1], wide) * scale
                weight = {q: cols[q][k] * scale for q in range(panel, groups)}
                across = weight[panel]
                below = jnp.where(index > k, across, 0.0)
                rows[panel] = jnp.where(index == k, pivot, rows[panel] - below * pivot)
                for j in range(k + 1, SUB):
                    factor = jnp.broadcast_to(across[j : j + 1], wide)
                    for q in range(panel, groups):
                        cols[q][j] = cols[q][j] - (below if q == panel else weight[q]) * factor
                for q in range(panel + 1, groups):
                    rows[q] = rows[q] - weight[q] * pivot
    return leaves


def factor_kernel(bound_ref, window_ref, bases_ref, upper_ref, work):
    columns, window_rows = window_ref.shape
    width = bases_ref.shape[1]
    group = lax.axis_index("child") * lax.axis_size("col") + lax.axis_index("col")
    bound = bound_ref[0]
    top = window_rows // 2 + window_rows // 16
    low = window_rows // 2 - window_rows // 16
    eye = jnp.where(
        lax.broadcasted_iota(jnp.int32, (columns, columns), 0)
        == lax.broadcasted_iota(jnp.int32, (columns, columns), 1),
        1.0,
        0.0,
    )
    lane = lax.broadcasted_iota(jnp.int32, (columns, window_rows), 1)
    window = window_ref[...]
    head = jnp.where(lane < bound, window, 0.0)
    tail = window - head
    spans = ((head, 0, (top + 127) // 128 * 128), (tail, low // 128 * 128, window_rows))
    counts = (bound, window_rows - bound)
    for leaf, (masked, start, stop) in enumerate(spans):
        part = masked[:, start:stop]
        gram = mm3(part, part, NT)
        work[leaf, :, :columns] = gram / counts[leaf].astype(jnp.float32)
        work[leaf, :, columns:] = eye
    small_eye = eye[:NB, :NB]
    for block in range(columns // NB):
        begin, end = block * NB, (block + 1) * NB
        aug = []
        for leaf in range(2):
            diagonal = jnp.concatenate([work[leaf, begin:end, begin:end], small_eye], axis=1)
            aug.append([diagonal[q * SUB : (q + 1) * SUB] for q in range(NB // SUB)])
        done = eliminate(aug)
        for leaf in range(2):
            inverse = jnp.concatenate(done[leaf], axis=0)[:, NB:]
            rows = mm(inverse, work[leaf, begin:end, :])
            work[leaf, begin:end, :] = rows
            if end < columns:
                work[leaf, end:, :] = work[leaf, end:, :] - mm3(rows[:, end:columns], rows, TN)
    keep = lax.broadcasted_iota(jnp.int32, (columns, columns), 1) >= lax.broadcasted_iota(
        jnp.int32, (columns, columns), 0
    )
    for leaf in range(2):
        upper_ref[leaf] = jnp.where(keep, work[leaf, :, :columns], 0.0)
    mine = pl.ds(pl.multiple_of(group * width, width), width)
    inverse = jnp.concatenate([work[0, mine, columns:], work[1, mine, columns:]], axis=0)
    both = mm3(inverse, window)
    lane = lax.broadcasted_iota(jnp.int32, (width, window_rows), 1)
    bases_ref[...] = jnp.where(lane < bound, both[:width], both[width:]).T


def factor(bound, window):
    columns, window_rows = window.shape
    width = columns // (2 * lax.axis_size("col"))
    return pl.pallas_call(
        factor_kernel,
        out_shape=(
            jax.ShapeDtypeStruct((window_rows, width), jnp.float32),
            jax.ShapeDtypeStruct((2, columns, columns), jnp.float32),
        ),
        in_specs=[SMEM, VMEM],
        out_specs=(VMEM, VMEM),
        scratch_shapes=[pltpu.VMEM((2, columns, 2 * columns), jnp.float32)],
        compiler_params=pltpu.CompilerParams(vmem_limit_bytes=48 << 20),
        name="factor",
    )(bound, window)


def couple_kernel(own_ref, sibling_ref, out_ref):
    width = out_ref.shape[2]
    group = lax.axis_index("child") * lax.axis_size("col") + lax.axis_index("col")
    mine = pl.ds(pl.multiple_of(group * width, width), width)
    for leaf in range(2):
        out_ref[0, leaf] = mm3(own_ref[leaf, mine, :], sibling_ref[leaf], NT)


def couple(own, sibling):
    columns = own.shape[1]
    width = columns // (2 * lax.axis_size("col"))
    return pl.pallas_call(
        couple_kernel,
        out_shape=jax.ShapeDtypeStruct((1, 2, width, columns), jnp.float32),
        in_specs=[VMEM, VMEM],
        out_specs=VMEM,
        name="couple",
    )(own, sibling)


def sibling_of(block):
    count = lax.axis_size("row")
    return lax.ppermute(block, "row", [(k, k ^ 1) for k in range(count)])


def local(contrib, assembled, pattern, omega, row_maps, leaf_bounds):
    tile_rows, tile_cols = contrib.shape[1:]
    window_rows = omega.shape[0]
    row_pos = lax.axis_index("row")
    col_pos = lax.axis_index("col")
    child_maps = row_maps[0]
    columns = lax.dynamic_slice_in_dim(child_maps, col_pos * tile_cols, tile_cols) - col_pos * window_rows
    targets = lax.dynamic_slice_in_dim(child_maps, row_pos * tile_rows, tile_rows) - row_pos * window_rows
    gathered = gather_rows(omega.T).reshape(-1, window_rows)
    part = sketch(pattern, gathered, contrib[0], assembled[0], columns[None, :], targets[:, None])
    window = reduce_windows(part)
    bases, upper = factor(leaf_bounds, window)
    coupling = couple(upper, sibling_of(upper))
    return (bases, coupling)


def solution(mesh):
    in_specs = (
        P("child", "row", "col"),
        P("child", "row", "col"),
        P("row", "col"),
        P("col", "row"),
        P("child", None),
        P("row"),
    )
    out_specs = (P("row", ("child", "col")), P("row", None, ("child", "col"), None))
    return jax.shard_map(local, mesh=mesh, in_specs=in_specs, out_specs=out_specs, check_vma=False)
```

time: 279 us -> 89.1 us (0.32)
  other arithmetic: 116 us -> 0.79 us
  waiting for transfers between devices: 89.9 us -> 13.4 us
  Pallas kernels: 0 us -> 65.7 us
  matrix products: 24.6 us -> 0 us
  local copies, waits for them, and re-layouts: 30.9 us -> 7.44 us
  between operations: 14.7 us -> 1.39 us
    another operation x16 -> x0, other arithmetic: 109 us -> none  [the longest x9 67 us: window_leaves(): factors = jnp.linalg.cholesky(jnp.stack([head_gram, tail_gram]) / counts)]
    pallas_call x0 -> x5, Pallas kernels: none -> 65.7 us  [the longest x1 25.3 us: gather_rows(): pl.pallas_call(gather_kernel, out_shape=jax.ShapeDtypeStruct((count,) + o...]
    all_gather x2 -> x0, waiting for transfers between devices: 53.7 us -> none  [the longest x1 29.4 us: local(): full_omega = lax.all_gather(omega, 'row', axis=1, tiled=True)]
    unnamed x4 -> x0, waiting for transfers between devices: 36.2 us -> none
    dot_general x5 -> x0, matrix products: 13.8 us -> none  [the longest x1 4.63 us: local(): sparse = jnp.dot(masked, full_omega, precision=highest)]
    ppermute x1, waiting for transfers between devices: 0.01 us -> 13.4 us  [sibling_of(): return lax.ppermute(block, 'row', [(k, k ^ 1) for k in range(count)])]
    another operation x18 -> x0, local copies, waits for them, and re-layouts: 10.8 us -> none  [the longest x7 5.21 us: window_leaves(): lax.linalg.triangular_solve(factors[0], head_rows, left_side=False, lower...]
    another operation x8 -> x0, matrix products: 10.8 us -> none  [the longest x3 4.21 us: window_leaves(): lax.linalg.triangular_solve(factors[1], tail_rows, left_side=False, lower...]
  transfers between devices with their start and end apart: 4 -> 1, of which waited for: 3 -> 1; matrix products, arithmetic and copies ran while one was open for 25% -> 1% of each run, Pallas kernels for 0% -> 0%
where the time goes in v1:
time: 89.1 us; the launch traced here: 88.8 us
  Pallas kernels  65.7 us (74%)
  waiting for transfers between devices  13.4 us (15%)
  local copies, waits for them, and re-layouts  7.44 us (8%)
  between operations  1.39 us (2%)
    pallas_call x1, Pallas kernels, gather_rows(): pl.pallas_call(gather_kernel, out_shape=jax.ShapeDtypeStruct((count,) + o...  25.3 us
    pallas_call x1, Pallas kernels, reduce_windows(): pl.pallas_call(reduce_kernel, out_shape=jax.ShapeDtypeStruct(part.shape,...  21.9 us
    ppermute x1, waiting for transfers between devices, sibling_of(): return lax.ppermute(block, 'row', [(k, k ^ 1) for k in range(count)])  13.4 us
    pallas_call x1, Pallas kernels, factor(): pl.pallas_call(factor_kernel, out_shape=(jax.ShapeDtypeStruct((window_row...  12.9 us
    unnamed x17, local copies, waits for them, and re-layouts  7.3 us
    pallas_call x1, Pallas kernels, sketch(): pl.pallas_call(sketch_kernel, out_shape=jax.ShapeDtypeStruct(omega.shape,...  3.44 us
    pallas_call x1, Pallas kernels, couple(): pl.pallas_call(couple_kernel, out_shape=jax.ShapeDtypeStruct((1, 2, width...  2.17 us
  transfers between devices with their start and end apart: 1, of which 1 were waited for; matrix products, arithmetic and copies ran while one was open for 1% of the time, Pallas kernels for 0%

profile of v1, /device:TPU:0, one launch (start us, length us, event | category | flops | bytes accessed | tf_op | source)
XLA Modules:
  0.0 88.8 jit_solution(34403765351785754)
XLA Ops:
  0.6 0.0 copy-start.4
  0.6 0.8 subtract_bitcast_fusion
  1.4 0.1 copy.9.targets_ref
  1.6 25.3 %gather_rows.1 = f32[4,64,1024]{2,1,0:T(8,128)} custom-call(f32[64,1024]{1,0:T(8,128)} %bitcast.13), custom_call_target="tpu_custom_call" | custom-call | tf_op jit(solution)/shard_map/gather_rows/pallas_call | solution.py:118
  26.9 0.0 copy-done.4
  27.0 0.0 copy-start.1
  27.0 1.2 %copy-done.1 = f32[4,64,1024]{2,1,0:T(8,128)S(1)} copy-done((f32[4,64,1024]{2,1,0:T(8,128)S(1)}, f32[4,64,1024]{2,1,0:T(8,128)}, u32[]{:S(2)}) %copy-start.1) | copy-done | bytes 1048600
  28.2 0.0 copy-start.3
  28.2 1.6 %copy-done.3 = f32[1,512,1024]{2,1,0:T(8,128)S(1)} copy-done((f32[1,512,1024]{2,1,0:T(8,128)S(1)}, f32[1,512,1024]{2,1,0:T(8,128)}, u32[]{:S(2)}) %copy-start.3) | copy-done | bytes 2097176
  29.8 0.0 copy-start.6
  29.8 0.7 copy-done.6
  30.5 3.4 %sketch.1 = f32[256,1024]{1,0:T(8,128)S(1)} custom-call(s32[4,4]{1,0:T(4,128)S(1)} %copy-done.6, f32[256,1024]{1,0:T(8,128)S(1)} %bitcast.9, f32[512,512]{1,0:T(8,128)S(1)} %bitcast.12, f32[512,1024]{1,0:T(8,128)S(1)} %bitcast.11, s32[1,512]{1,0:T(1,128)S(1)} %get-tuple-element.11.columns_ref, s32[512,1]{1,0:T(8,128)S(1)} %copy.9.targets_ref), custom_call_target="tpu_custom_call" | custom-call | tf_op jit(solution)/shard_map/sketch/pallas_call | solution.py:165
  33.9 0.0 copy-start.2
  33.9 1.0 %copy-done.2 = f32[256,1024]{1,0:T(8,128)} copy-done((f32[256,1024]{1,0:T(8,128)}, f32[256,1024]{1,0:T(8,128)S(1)}, u32[]{:S(2)}) %copy-start.2) | copy-done | bytes 1048600
  34.9 21.9 %reduce_windows.1 = f32[4,2,32,1024]{3,2,1,0:T(8,128)} custom-call(f32[4,2,32,1024]{3,2,1,0:T(8,128)} %bitcast.10), custom_call_target="tpu_custom_call" | custom-call | tf_op jit(solution)/shard_map/reduce_windows/pallas_call | solution.py:259
  57.4 0.0 copy-start
  57.4 1.2 %copy-done = f32[4,2,32,1024]{3,2,1,0:T(8,128)S(1)} copy-done((f32[4,2,32,1024]{3,2,1,0:T(8,128)S(1)}, f32[4,2,32,1024]{3,2,1,0:T(8,128)}, u32[]{:S(2)}) %copy-start) | copy-done | bytes 1048600
  58.6 12.9 %factor.1 = (f32[1024,32]{1,0:T(8,128)S(1)}, f32[2,256,256]{2,1,0:T(8,128)S(1)}) custom-call(s32[1]{0:T(128)S(6)} %copy.11.bound_ref, f32[256,1024]{1,0:T(8,128)S(1)} %bitcast.8), custom_call_target="tpu_custom_call" | custom-call | tf_op jit(solution)/shard_map/factor/pallas_call | solution.py:356
  71.5 0.0 copy-start.5
  71.5 0.1 collective-permute-start
  71.6 0.8 copy.10
  72.4 13.4 %collective-permute-done.sibling_ref = f32[2,256,256]{2,1,0:T(8,128)S(1)} collective-permute-done((f32[2,256,256]{2,1,0:T(8,128)S(1)}, f32[2,256,256]{2,1,0:T(8,128)S(1)}, u32[]{:S(2)}, u32[]{:S(2)}) %collective-permute-start) | collective-permute-done | bytes 524320 | tf_op jit(solution)/shard_map/ppermute | solution.py:392
  85.8 0.0 copy-done.5
  85.8 0.0 copy-start.7
  85.8 0.8 copy-done.7
  86.6 2.2 %couple.1 = f32[1,2,32,256]{3,2,1,0:T(8,128)} custom-call(f32[2,256,256]{2,1,0:T(8,128)} %copy-done.5, f32[2,256,256]{2,1,0:T(8,128)} %copy-done.7), custom_call_target="tpu_custom_call" | custom-call | tf_op jit(solution)/shard_map/couple/pallas_call | solution.py:381
Async XLA Ops:
  0.6 26.3 %copy-start.4 = (f32[1,512,512]{2,1,0:T(8,128)S(1)}, f32[1,512,512]{2,1,0:T(8,128)}, u32[]{:S(2)}) copy-start(f32[1,512,512]{2,1,0:T(8,128)} %param.6) | copy-start | bytes 3145732
  27.0 1.2 %copy-start.1 = (f32[4,64,1024]{2,1,0:T(8,128)S(1)}, f32[4,64,1024]{2,1,0:T(8,128)}, u32[]{:S(2)}) copy-start(f32[4,64,1024]{2,1,0:T(8,128)} %gather_rows.1) | copy-start | bytes 3145732
  28.2 1.6 %copy-start.3 = (f32[1,512,1024]{2,1,0:T(8,128)S(1)}, f32[1,512,1024]{2,1,0:T(8,128)}, u32[]{:S(2)}) copy-start(f32[1,512,1024]{2,1,0:T(8,128)} %param.7) | copy-start | bytes 6291460
  29.8 0.7 copy-start.6
  33.9 1.0 %copy-start.2 = (f32[256,1024]{1,0:T(8,128)}, f32[256,1024]{1,0:T(8,128)S(1)}, u32[]{:S(2)}) copy-start(f32[256,1024]{1,0:T(8,128)S(1)} %sketch.1) | copy-start | bytes 3145732
  57.4 1.2 %copy-start = (f32[4,2,32,1024]{3,2,1,0:T(8,128)S(1)}, f32[4,2,32,1024]{3,2,1,0:T(8,128)}, u32[]{:S(2)}) copy-start(f32[4,2,32,1024]{3,2,1,0:T(8,128)} %reduce_windows.1) | copy-start | bytes 3145732
  71.5 14.3 %copy-start.5 = (f32[2,256,256]{2,1,0:T(8,128)}, f32[2,256,256]{2,1,0:T(8,128)S(1)}, u32[]{:S(2)}) copy-start(f32[2,256,256]{2,1,0:T(8,128)S(1)} %get-tuple-element.5.own_ref) | copy-start | bytes 1572868
  71.5 14.3 %collective-permute-start = (f32[2,256,256]{2,1,0:T(8,128)S(1)}, f32[2,256,256]{2,1,0:T(8,128)S(1)}, u32[]{:S(2)}, u32[]{:S(2)}) collective-permute-start(f32[2,256,256]{2,1,0:T(8,128)S(1)} %get-tuple-element.5.own_ref), channel_id=1, source_target_pairs={{0,4},{4,0},{8,12},{12,8},{1,5},{5,1},{9,13},{13,9},{2,6},{6,2},{1... | collective-permute-start | bytes 1572872 | tf_op jit(solution)/shard_map/ppermute | solution.py:392
  85.8 0.8 copy-start.7

commit v2 on v1

v2 whole, which is shorter than its diff:
```python
import jax
import jax.numpy as jnp
from jax import lax
from jax.experimental import pallas as pl
from jax.experimental.pallas import tpu as pltpu
from jax.sharding import PartitionSpec as P

BT = 256
NB = 64
SUB = 8
MESH = pl.DeviceIdType.MESH
highest = lax.Precision.HIGHEST
VMEM = pl.BlockSpec(memory_space=pltpu.VMEM)
SMEM = pl.BlockSpec(memory_space=pltpu.SMEM)

NN = (((1,), (0,)), ((), ()))
NT = (((1,), (1,)), ((), ()))
TN = (((0,), (0,)), ((), ()))


def mm(a, b, dims=NN):
    return lax.dot_general(a, b, dims, precision=highest, preferred_element_type=jnp.float32)


def split(a):
    high = a.astype(jnp.bfloat16)
    low = (a - high.astype(jnp.float32)).astype(jnp.bfloat16)
    return high, low


def dot16(a, b, dims=NN):
    return lax.dot_general(a, b, dims, preferred_element_type=jnp.float32)


def mm3(a, b, dims=NN):
    (ah, al), (bh, bl) = split(a), split(b)
    return dot16(ah, bh, dims) + (dot16(ah, bl, dims) + dot16(al, bh, dims))


class Plane:
    def __init__(self):
        self.cols = lax.axis_size("col")
        self.chips = self.cols * lax.axis_size("child") // 2
        self.group = lax.axis_index("child") * self.cols + lax.axis_index("col")
        self.chip = self.group // 2
        self.core = self.group % 2
        self.order = [lax.rem(self.chip + step, self.chips) for step in range(self.chips)]

    def device(self, chip, core):
        flat = chip * 2 + core
        return {"child": flat // self.cols, "col": flat % self.cols}


def remote(source, target, send_sem, recv_sem, device):
    return pltpu.make_async_remote_copy(
        src_ref=source, dst_ref=target, send_sem=send_sem, recv_sem=recv_sem, device_id=device, device_id_type=MESH
    )


def greet(plane):
    count = lax.axis_size("row")
    me = lax.axis_index("row")
    barrier = pltpu.get_barrier_semaphore()

    @pl.when(me > 0)
    def _():
        pl.semaphore_signal(barrier, inc=1, device_id={"row": me - 1}, device_id_type=MESH)

    @pl.when(me < count - 1)
    def _():
        pl.semaphore_signal(barrier, inc=1, device_id={"row": me + 1}, device_id_type=MESH)

    pl.semaphore_signal(barrier, inc=1, device_id=plane.device(plane.chip, 1 - plane.core), device_id_type=MESH)
    for step in range(1, plane.chips):
        pl.semaphore_signal(
            barrier, inc=1, device_id=plane.device(plane.order[step], plane.core), device_id_type=MESH
        )
    pl.semaphore_wait(barrier, plane.chips + jnp.minimum(me, 1) + jnp.minimum(count - 1 - me, 1))


def gather(own_ref, out_ref, sems, prepare):
    send_right, send_left, recv, swap_send, swap_recv, local_sem = sems
    count = lax.axis_size("row")
    me = lax.axis_index("row")
    half = lax.axis_index("child")
    has_left = me > 0
    has_right = me < count - 1
    keep = pltpu.make_async_copy(own_ref, out_ref.at[me], local_sem)
    keep.start()

    def hop(block, target, step, send):
        source = own_ref.at[half] if step == 0 else out_ref.at[block, half]
        return remote(source, out_ref.at[block, half], send.at[block], recv.at[block], {"row": target})

    def swap(block):
        place = out_ref.at[block, half]
        return remote(place, place, swap_send.at[block], swap_recv.at[block], {"child": 1 - half})

    for step in range(count):
        low = me - step
        high = me + step
        if step > 0:

            @pl.when(low >= 0)
            def _():
                hop(low, me - 1, step, send_right).wait_recv()

        @pl.when(jnp.logical_and(low >= 0, has_right))
        def _():
            hop(low, me + 1, step, send_right).start()

        if step > 0:

            @pl.when(low >= 0)
            def _():
                swap(low).start()

            @pl.when(high < count)
            def _():
                hop(high, me + 1, step, send_left).wait_recv()

        @pl.when(jnp.logical_and(high < count, has_left))
        def _():
            hop(high, me - 1, step, send_left).start()

        if step > 0:

            @pl.when(high < count)
            def _():
                swap(high).start()

        if step == 0:
            prepare()

    keep.wait()
    for step in range(1, count):
        block = lax.rem(me + step, count)
        place = out_ref.at[block, 1 - half]
        remote(place, place, swap_send.at[block], swap_recv.at[block], {"child": 1 - half}).wait_recv()

    def drain():
        for step in range(count):
            low = me - step
            high = me + step

            @pl.when(jnp.logical_and(low >= 0, has_right))
            def _():
                hop(low, me + 1, step, send_right).wait_send()

            @pl.when(jnp.logical_and(high < count, has_left))
            def _():
                hop(high, me - 1, step, send_left).wait_send()

        for step in range(1, count):
            swap(lax.rem(me + step, count)).wait_send()

    return drain


def prepare_sketch(pattern_ref, contrib, assembled, columns_ref, targets_ref, held):
    pick, place, front, entries = held
    half = lax.axis_index("child")
    tile_rows, tile_cols = contrib.shape
    window_rows = assembled.shape[1]
    lanes = lax.broadcasted_iota(jnp.int32, (window_rows, tile_cols), 0)
    pick[...] = jnp.where(lanes == columns_ref[...], 1.0, 0.0).astype(jnp.bfloat16)
    rows = lax.broadcasted_iota(jnp.int32, (tile_rows, window_rows), 1)
    place[...] = jnp.where(rows == targets_ref[...], 1.0, 0.0).astype(jnp.bfloat16)
    front[0], front[1] = split(contrib[...])
    for row in range(tile_rows // BT):
        for col in range(window_rows // BT):
            where = (slice(row * BT, (row + 1) * BT), slice(col * BT, (col + 1) * BT))
            present = pattern_ref[half * (tile_rows // BT) + row, col].astype(jnp.float32)
            entries[(0,) + where], entries[(1,) + where] = split(assembled[where] * present)


def sketch(omega, held, part_ref):
    pick, place, front, entries = held
    half = lax.axis_index("child")
    tile_rows = place.shape[0]
    omega_high, omega_low = split(omega)
    picked_high = dot16(omega_high, pick[...]).astype(jnp.bfloat16)
    picked_low = dot16(omega_low, pick[...]).astype(jnp.bfloat16)
    product = dot16(picked_high, front[0], NT) + (
        dot16(picked_high, front[1], NT) + dot16(picked_low, front[0], NT)
    )
    sparse = dot16(omega_high, entries[0], NT) + (
        dot16(omega_high, entries[1], NT) + dot16(omega_low, entries[0], NT)
    )
    product_high, product_low = split(product)
    part_ref[...] = (dot16(product_high, place[...]) + dot16(product_low, place[...])).reshape(part_ref.shape)
    where = pl.ds(pl.multiple_of(half * tile_rows, tile_rows), tile_rows)
    part_ref[:, :, :, where] = part_ref[:, :, :, where] + sparse.reshape(part_ref.shape[:3] + (tile_rows,))


def reduce(plane, part_ref, out_ref, pair_buf, sum_buf, chip_buf, sems):
    pair_send, pair_recv, chip_send, chip_recv, all_send, all_recv, last_send, last_recv = sems
    chips, chip, core, order = plane.chips, plane.chip, plane.core, plane.order
    other = 1 - core
    partner = plane.device(chip, other)

    def copy(source, target, send, recv, index, device, recv_index):
        return remote(source, target, send.at[index], recv.at[recv_index], device)

    steps = list(range(1, chips)) + [0]
    pair = {}
    for step in steps:
        c = order[step]
        pair[step] = copy(part_ref.at[c, other], pair_buf.at[c], pair_send, pair_recv, c, partner, c)
        pair[step].start()
    sends = {}
    for step in range(1, chips):
        c = order[step]
        pair[step].wait_recv()
        sum_buf[c] = part_ref[c, core] + pair_buf[c]
        sends[step] = copy(sum_buf.at[c], chip_buf.at[chip], chip_send, chip_recv, c, plane.device(c, core), chip)
        sends[step].start()
    pair[0].wait_recv()
    total = part_ref[chip, core] + pair_buf[chip]
    for step in range(1, chips):
        c = order[step]
        copy(sum_buf.at[c], chip_buf.at[c], chip_send, chip_recv, c, plane.device(c, core), c).wait_recv()
        total = total + chip_buf[c]
    out_ref[chip, core] = total
    own = out_ref.at[chip, core]
    spread = {}
    for step in range(1, chips):
        c = order[step]
        spread[step] = copy(own, own, all_send, all_recv, c, plane.device(c, core), chip)
        spread[step].start()
    last = {}
    last[0] = copy(own, own, last_send, last_recv, chip, partner, chip)
    last[0].start()
    for step in range(1, chips):
        c = order[step]
        block = out_ref.at[c, core]
        copy(block, block, all_send, all_recv, c, plane.device(c, core), c).wait_recv()
        last[step] = copy(block, block, last_send, last_recv, c, partner, c)
        last[step].start()
    for step in range(chips):
        c = order[step]
        block = out_ref.at[c, other]
        copy(block, block, last_send, last_recv, c, partner, c).wait_recv()

    def drain():
        for step in range(chips):
            pair[step].wait_send()
            last[step].wait_send()
        for step in range(1, chips):
            sends[step].wait_send()
            spread[step].wait_send()

    return drain


def eliminate(leaves):
    groups = NB // SUB
    index = lax.broadcasted_iota(jnp.int32, (SUB, 2 * NB), 0)
    wide = (SUB, 2 * NB)
    leaves = [list(rows) for rows in leaves]
    for panel in range(groups):
        first = panel * SUB
        columns = [
            {
                q: [jnp.broadcast_to(rows[q][:, first + k : first + k + 1], wide) for k in range(SUB)]
                for q in range(panel, groups)
            }
            for rows in leaves
        ]
        for k in range(SUB):
            for rows, cols in zip(leaves, columns):
                own = cols[panel]
                scale = lax.rsqrt(jnp.broadcast_to(own[k][k : k + 1], wide))
                pivot = jnp.broadcast_to(rows[panel][k : k + 1], wide) * scale
                weight = {q: cols[q][k] * scale for q in range(panel, groups)}
                across = weight[panel]
                below = jnp.where(index > k, across, 0.0)
                rows[panel] = jnp.where(index == k, pivot, rows[panel] - below * pivot)
                for j in range(k + 1, SUB):
                    factor = jnp.broadcast_to(across[j : j + 1], wide)
                    for q in range(panel, groups):
                        cols[q][j] = cols[q][j] - (below if q == panel else weight[q]) * factor
                for q in range(panel + 1, groups):
                    rows[q] = rows[q] - weight[q] * pivot
    return leaves


def factor(bound, window, work, done_block):
    columns, window_rows = window.shape
    top = window_rows // 2 + window_rows // 16
    low = window_rows // 2 - window_rows // 16
    eye = jnp.where(
        lax.broadcasted_iota(jnp.int32, (columns, columns), 0)
        == lax.broadcasted_iota(jnp.int32, (columns, columns), 1),
        1.0,
        0.0,
    )
    lane = lax.broadcasted_iota(jnp.int32, (columns, window_rows), 1)
    head = jnp.where(lane < bound, window, 0.0)
    tail = window - head
    spans = ((head, 0, (top + 127) // 128 * 128), (tail, low // 128 * 128, window_rows))
    counts = (bound, window_rows - bound)
    for leaf, (masked, start, stop) in enumerate(spans):
        part = masked[:, start:stop]
        gram = mm3(part, part, NT)
        work[leaf, :, :columns] = gram / counts[leaf].astype(jnp.float32)
        work[leaf, :, columns:] = eye
    small_eye = eye[:NB, :NB]
    for block in range(columns // NB):
        begin, end = block * NB, (block + 1) * NB
        aug = []
        for leaf in range(2):
            diagonal = jnp.concatenate([work[leaf, begin:end, begin:end], small_eye], axis=1)
            aug.append([diagonal[q * SUB : (q + 1) * SUB] for q in range(NB // SUB)])
        done = eliminate(aug)
        for leaf in range(2):
            inverse = jnp.concatenate(done[leaf], axis=0)[:, NB:]
            rows = mm(inverse, work[leaf, begin:end, :])
            work[leaf, begin:end, :] = rows
            done_block(leaf, block, begin, end, rows[:, :columns])
            if end < columns:
                work[leaf, end:, :] = work[leaf, end:, :] - mm3(rows[:, end:columns], rows, TN)


def whole_kernel(
    bound_ref, pattern_ref, omega_ref, contrib_ref, assembled_ref, columns_ref, targets_ref, bases_ref, coupling_ref,
    gathered, contrib_buf, assembled_buf, pick, place, front, entries,
    part, window, pair_buf, sum_buf, chip_buf, work, upper, sibling, input_sems, *sems,
):
    plane = Plane()
    window_rows = assembled_buf.shape[1]
    columns, width = upper.shape[1], bases_ref.shape[0]
    held = (pick, place, front, entries)
    load_front = pltpu.make_async_copy(contrib_ref.at[0], contrib_buf, input_sems.at[0])
    load_entries = pltpu.make_async_copy(assembled_ref.at[0], assembled_buf, input_sems.at[1])
    load_front.start()
    load_entries.start()
    greet(plane)

    def prepare():
        load_front.wait()
        load_entries.wait()
        prepare_sketch(pattern_ref, contrib_buf, assembled_buf, columns_ref, targets_ref, held)

    drain_gather = gather(omega_ref, gathered, sems[:6], prepare)
    sketch(gathered[...].reshape(columns, window_rows), held, part)
    drain_reduce = reduce(plane, part, window, pair_buf, sum_buf, chip_buf, sems[6:14])
    drain_gather()
    drain_reduce()

    near_send, near_recv = sems[14:]
    row_pos = lax.axis_index("row")
    near = {"row": row_pos + 1 - 2 * (row_pos % 2)}

    def send(leaf, block):
        start = block * NB // 128 * 128
        rows = slice(block * NB, (block + 1) * NB)
        source, target = upper.at[leaf, rows, start:], sibling.at[leaf, rows, start:]
        return remote(source, target, near_send.at[leaf, block], near_recv.at[leaf, block], near)

    def done_block(leaf, block, begin, end, rows):
        keep = lax.broadcasted_iota(jnp.int32, rows.shape, 1) >= begin + lax.broadcasted_iota(
            jnp.int32, rows.shape, 0
        )
        upper[leaf, begin:end, :] = jnp.where(keep, rows, 0.0)
        send(leaf, block).start()

    bound = bound_ref[0]
    samples = window[...].reshape(columns, window_rows)
    factor(bound, samples, work, done_block)
    mine = pl.ds(pl.multiple_of(plane.group * width, width), width)
    inverse = jnp.concatenate([work[0, mine, columns:], work[1, mine, columns:]], axis=0)
    both = mm3(inverse, samples)
    lane = lax.broadcasted_iota(jnp.int32, (width, window_rows), 1)
    bases_ref[...] = jnp.where(lane < bound, both[:width], both[width:])
    for leaf in range(2):
        own = upper[leaf, mine, :]
        pieces = []
        for block in range(columns // NB):
            start = block * NB // 128 * 128
            send(leaf, block).wait_recv()
            pieces.append(mm3(own[:, start:], sibling[leaf, block * NB : (block + 1) * NB, start:], NT))
        coupling_ref[0, leaf] = jnp.concatenate(pieces, axis=1)
    for leaf in range(2):
        for block in range(columns // NB):
            send(leaf, block).wait_send()


def local(contrib, assembled, pattern, omega, row_maps, leaf_bounds):
    tile_rows, tile_cols = contrib.shape[1:]
    window_rows, own_width = omega.shape
    rows = lax.axis_size("row")
    chips = lax.axis_size("col") * lax.axis_size("child") // 2
    columns = own_width * rows
    width = columns // (2 * chips)
    row_pos = lax.axis_index("row")
    col_pos = lax.axis_index("col")
    child_maps = row_maps[0]
    col_maps = lax.dynamic_slice_in_dim(child_maps, col_pos * tile_cols, tile_cols) - col_pos * window_rows
    targets = lax.dynamic_slice_in_dim(child_maps, row_pos * tile_rows, tile_rows) - row_pos * window_rows
    own = omega.T.reshape(2, own_width // 2, window_rows)
    f32, bf16, dma = jnp.float32, jnp.bfloat16, pltpu.SemaphoreType.DMA
    any_space = pl.BlockSpec(memory_space=pl.ANY)
    block = pltpu.VMEM((chips, width, window_rows), f32)
    split_window = pltpu.VMEM((chips, 2, width, window_rows), f32)
    bases, coupling = pl.pallas_call(
        whole_kernel,
        out_shape=(
            jax.ShapeDtypeStruct((width, window_rows), f32),
            jax.ShapeDtypeStruct((1, 2, width, columns), f32),
        ),
        in_specs=[SMEM, SMEM, VMEM, any_space, any_space, VMEM, VMEM],
        out_specs=(VMEM, VMEM),
        scratch_shapes=[
            pltpu.VMEM((rows, 2, own_width // 2, window_rows), f32),
            pltpu.VMEM((tile_rows, tile_cols), f32),
            pltpu.VMEM((tile_rows, window_rows), f32),
            pltpu.VMEM((window_rows, tile_cols), bf16),
            pltpu.VMEM((tile_rows, window_rows), bf16),
            pltpu.VMEM((2, tile_rows, tile_cols), bf16),
            pltpu.VMEM((2, tile_rows, window_rows), bf16),
            split_window,
            split_window,
            block,
            block,
            block,
            pltpu.VMEM((2, columns, 2 * columns), f32),
            pltpu.VMEM((2, columns, columns), f32),
            pltpu.VMEM((2, columns, columns), f32),
            dma((2,)),
        ]
        + [dma((rows,))] * 5
        + [dma]
        + [dma((chips,))] * 8
        + [dma((2, columns // NB))] * 2,
        compiler_params=pltpu.CompilerParams(
            collective_id=0, has_side_effects=True, vmem_limit_bytes=56 << 20
        ),
        name="front_samples",
    )(leaf_bounds, pattern, own, contrib, assembled, col_maps[None, :], targets[:, None])
    return (bases.T, coupling)


def solution(mesh):
    in_specs = (
        P("child", "row", "col"),
        P("child", "row", "col"),
        P("row", "col"),
        P("col", "row"),
        P("child", None),
        P("row"),
    )
    out_specs = (P("row", ("child", "col")), P("row", None, ("child", "col"), None))
    return jax.shard_map(local, mesh=mesh, in_specs=in_specs, out_specs=out_specs, check_vma=False)
```

time: 89.1 us -> 65.4 us (0.73)
  waiting for transfers between devices: 13.4 us -> 0 us
  Pallas kernels: 65.7 us -> 58.6 us
  local copies, waits for them, and re-layouts: 7.44 us -> 3.89 us
    ppermute x1 -> x0, waiting for transfers between devices: 13.4 us -> none  [sibling_of(): return lax.ppermute(block, 'row', [(k, k ^ 1) for k in range(count)])]
    pallas_call x5 -> x1, Pallas kernels: 65.7 us -> 58.6 us  [local(): pl.pallas_call(whole_kernel, out_shape=(jax.ShapeDtypeStruct((width, wind...]
    unnamed x17 -> x2, local copies, waits for them, and re-layouts: 7.3 us -> 3.04 us
  transfers between devices with their start and end apart: 1 -> 0, of which waited for: 1 -> 0; matrix products, arithmetic and copies ran while one was open for 1% -> 0% of each run, Pallas kernels for 0% -> 0%
where the time goes in v2:
time: 65.4 us; the launch traced here: 65.1 us
  Pallas kernels  58.6 us (90%)
  local copies, waits for them, and re-layouts  3.89 us (6%)
  other arithmetic  1.34 us (2%)
  between operations  1.29 us (2%)
    pallas_call x1, Pallas kernels, local(): pl.pallas_call(whole_kernel, out_shape=(jax.ShapeDtypeStruct((width, wind...  58.6 us
    unnamed x2, local copies, waits for them, and re-layouts  3.04 us
    sub x1, other arithmetic, local(): lax.dynamic_slice_in_dim(child_maps, row_pos * tile_rows, tile_rows)  1.34 us

profile of v2, /device:TPU:0, one launch (start us, length us, event | category | flops | bytes accessed | tf_op | source)
XLA Modules:
  0.0 65.1 jit_solution(15953803937633987582)
XLA Ops:
  1.3 1.3 %subtract_bitcast_fusion = (s32[512,1]{0,1:T(1,128)S(1)}, s32[1,512]{1,0:T(1,128)}) fusion(s32[1,2048]{1,0:T(1,128)} %param.10, s32[]{:T(128)S(6)} %select_n.7, s32[]{:T(128)S(6)} %mul.15, s32[]{:T(128)S(6)} %mul.13, s32[]{:T(128)S(6)} %select_n.6), kind=kLoop, calls=%fused_computation | loop fusion | flops 1024 | bytes 8208 | tf_op jit(solution)/shard_map/sub | solution.py:400
  2.6 0.8 %copy.8.targets_ref = s32[512,1]{1,0:T(8,128)} copy(s32[512,1]{0,1:T(1,128)S(1)} %get-tuple-element.6) | data formatting | bytes 4096 | tf_op jit(solution)/shard_map/sub | solution.py:400
  3.5 58.6 %front_samples.1 = (f32[32,1024]{1,0:T(8,128)}, f32[1,2,32,256]{3,2,1,0:T(8,128)}) custom-call(s32[1]{0:T(128)S(6)} %copy.11.bound_ref, s32[4,4]{1,0:T(4,128)} %pattern_ref.1, f32[2,32,1024]{2,1,0:T(8,128)} %bitcast.6, f32[1,512,512]{2,1,0:T(8,128)} %contrib_ref.1, f32[1,512,1024]{2,1,0:T(8,128)} %assembled_ref.1, s32[1,512]{1,0:T(1,128)} %get-tuple-element.7.columns_ref, ...), custom_call_target="tpu_custom_call" | custom-call | tf_op jit(solution)/shard_map/front_samples/pallas_call | solution.py:406
  62.1 1.6 %copy.12 = f32[1024,32]{0,1:T(8,128)} copy(f32[1024,32]{0,1:T(8,128)} %bitcast.7) | data formatting | bytes 262144
  63.7 1.5 %copy.13 = f32[1,2,32,256]{3,2,1,0:T(8,128)} copy(f32[1,2,32,256]{3,2,1,0:T(8,128)} %get-tuple-element.11) | data formatting | bytes 131072

commit v3 on v2

--- a/solution.py
+++ b/solution.py
@@ -78,7 +78,7 @@
     pl.semaphore_wait(barrier, plane.chips + jnp.minimum(me, 1) + jnp.minimum(count - 1 - me, 1))
 
 
-def gather(own_ref, out_ref, sems, prepare):
+def gather(own_ref, out_ref, sems, prepare, stage, settle):
     send_right, send_left, recv, swap_send, swap_recv, local_sem = sems
     count = lax.axis_size("row")
     me = lax.axis_index("row")
@@ -96,6 +96,21 @@
         place = out_ref.at[block, half]
         return remote(place, place, swap_send.at[block], swap_recv.at[block], {"child": 1 - half})
 
+    def at_distance(step, act):
+        for block, there in ((me - step, me >= step), (me + step, me + step < count)):
+
+            @pl.when(there)
+            def _():
+                act(block)
+
+    def wait_swap(block):
+        place = out_ref.at[block, 1 - half]
+        remote(place, place, swap_send.at[block], swap_recv.at[block], {"child": 1 - half}).wait_recv()
+
+    def staged(block):
+        wait_swap(block)
+        stage(block)
+
     for step in range(count):
         low = me - step
         high = me + step
@@ -131,12 +146,21 @@
 
         if step == 0:
             prepare()
-
-    keep.wait()
-    for step in range(1, count):
-        block = lax.rem(me + step, count)
-        place = out_ref.at[block, 1 - half]
-        remote(place, place, swap_send.at[block], swap_recv.at[block], {"child": 1 - half}).wait_recv()
+            keep.wait()
+            stage(me)
+        else:
+            if step > 1:
+                at_distance(step - 1, staged)
+            if step == 2:
+                settle(me)
+            if step > 2:
+                at_distance(step - 2, settle)
+    at_distance(count - 1, staged)
+    if count == 2:
+        settle(me)
+    if count > 2:
+        at_distance(count - 2, settle)
+    at_distance(count - 1, settle)
 
     def drain():
         for step in range(count):
@@ -174,83 +198,94 @@
             entries[(0,) + where], entries[(1,) + where] = split(assembled[where] * present)
 
 
+def stacked(a, b, dims=NN):
+    rows = a.shape[0] // 2
+    both = dot16(a, b[0], dims)
+    return both[:rows] + (dot16(a[:rows], b[1], dims) + both[rows:])
+
+
 def sketch(omega, held, part_ref):
     pick, place, front, entries = held
     half = lax.axis_index("child")
-    tile_rows = place.shape[0]
-    omega_high, omega_low = split(omega)
-    picked_high = dot16(omega_high, pick[...]).astype(jnp.bfloat16)
-    picked_low = dot16(omega_low, pick[...]).astype(jnp.bfloat16)
-    product = dot16(picked_high, front[0], NT) + (
-        dot16(picked_high, front[1], NT) + dot16(picked_low, front[0], NT)
-    )
-    sparse = dot16(omega_high, entries[0], NT) + (
-        dot16(omega_high, entries[1], NT) + dot16(omega_low, entries[0], NT)
-    )
-    product_high, product_low = split(product)
-    part_ref[...] = (dot16(product_high, place[...]) + dot16(product_low, place[...])).reshape(part_ref.shape)
+    rows, tile_rows = omega.shape[0], place.shape[0]
+    both = jnp.concatenate(split(omega), axis=0)
+    picked = dot16(both, pick[...]).astype(jnp.bfloat16)
+    product = stacked(picked, front, NT)
+    sparse = stacked(both, entries, NT)
+    spread = dot16(jnp.concatenate(split(product), axis=0), place[...])
+    part_ref[...] = (spread[:rows] + spread[rows:]).reshape(part_ref.shape)
     where = pl.ds(pl.multiple_of(half * tile_rows, tile_rows), tile_rows)
     part_ref[:, :, :, where] = part_ref[:, :, :, where] + sparse.reshape(part_ref.shape[:3] + (tile_rows,))
 
 
-def reduce(plane, part_ref, out_ref, pair_buf, sum_buf, chip_buf, sems):
-    pair_send, pair_recv, chip_send, chip_recv, all_send, all_recv, last_send, last_recv = sems
-    chips, chip, core, order = plane.chips, plane.chip, plane.core, plane.order
-    other = 1 - core
-    partner = plane.device(chip, other)
-
-    def copy(source, target, send, recv, index, device, recv_index):
-        return remote(source, target, send.at[index], recv.at[recv_index], device)
-
-    steps = list(range(1, chips)) + [0]
-    pair = {}
-    for step in steps:
-        c = order[step]
-        pair[step] = copy(part_ref.at[c, other], pair_buf.at[c], pair_send, pair_recv, c, partner, c)
-        pair[step].start()
-    sends = {}
-    for step in range(1, chips):
-        c = order[step]
-        pair[step].wait_recv()
-        sum_buf[c] = part_ref[c, core] + pair_buf[c]
-        sends[step] = copy(sum_buf.at[c], chip_buf.at[chip], chip_send, chip_recv, c, plane.device(c, core), chip)
-        sends[step].start()
-    pair[0].wait_recv()
-    total = part_ref[chip, core] + pair_buf[chip]
-    for step in range(1, chips):
-        c = order[step]
-        copy(sum_buf.at[c], chip_buf.at[c], chip_send, chip_recv, c, plane.device(c, core), c).wait_recv()
-        total = total + chip_buf[c]
-    out_ref[chip, core] = total
-    own = out_ref.at[chip, core]
-    spread = {}
-    for step in range(1, chips):
-        c = order[step]
-        spread[step] = copy(own, own, all_send, all_recv, c, plane.device(c, core), chip)
-        spread[step].start()
-    last = {}
-    last[0] = copy(own, own, last_send, last_recv, chip, partner, chip)
-    last[0].start()
-    for step in range(1, chips):
-        c = order[step]
-        block = out_ref.at[c, core]
-        copy(block, block, all_send, all_recv, c, plane.device(c, core), c).wait_recv()
-        last[step] = copy(block, block, last_send, last_recv, c, partner, c)
-        last[step].start()
-    for step in range(chips):
-        c = order[step]
-        block = out_ref.at[c, other]
-        copy(block, block, last_send, last_recv, c, partner, c).wait_recv()
-
-    def drain():
-        for step in range(chips):
-            pair[step].wait_send()
-            last[step].wait_send()
-        for step in range(1, chips):
-            sends[step].wait_send()
-            spread[step].wait_send()
-
-    return drain
+class Reduce:
+    def __init__(self, plane, part_ref, out_ref, pair_buf, sum_buf, chip_buf, sems):
+        self.plane, self.part, self.out = plane, part_ref, out_ref
+        self.pair_buf, self.sum_buf, self.chip_buf, self.sems = pair_buf, sum_buf, chip_buf, sems
+        self.partner = plane.device(plane.chip, 1 - plane.core)
+
+    def pair(self, r):
+        source = self.part.at[r, :, 1 - self.plane.core]
+        return remote(source, self.pair_buf.at[r], self.sems[0].at[r], self.sems[1].at[r], self.partner)
+
+    def give(self, r, c):
+        chip = self.plane.chip
+        device = self.plane.device(c, self.plane.core)
+        return remote(
+            self.sum_buf.at[r, c], self.chip_buf.at[r, chip], self.sems[2].at[r, c], self.sems[3].at[r, chip], device
+        )
+
+    def take(self, r, c):
+        device = self.plane.device(c, self.plane.core)
+        return remote(self.sum_buf.at[r, c], self.chip_buf.at[r, c], self.sems[2].at[r, c], self.sems[3].at[r, c], device)
+
+    def show(self, r, c, owner):
+        block = self.out.at[r, owner, self.plane.core]
+        device = self.plane.device(c, self.plane.core)
+        return remote(block, block, self.sems[4].at[r, c], self.sems[5].at[r, owner], device)
+
+    def hand(self, r, c, core):
+        block = self.out.at[r, c, core]
+        return remote(block, block, self.sems[6].at[r, c], self.sems[7].at[r, c], self.partner)
+
+    def begin(self, r):
+        self.pair(r).start()
+
+    def settle(self, r):
+        plane = self.plane
+        self.pair(r).wait_recv()
+        for c in plane.order[1:]:
+            self.sum_buf[r, c] = self.part[r, c, plane.core] + self.pair_buf[r, c]
+            self.give(r, c).start()
+
+    def finish(self, stages):
+        plane = self.plane
+        chip, core, others = plane.chip, plane.core, plane.order[1:]
+        for r in stages:
+            total = self.part[r, chip, core] + self.pair_buf[r, chip]
+            for c in others:
+                self.take(r, c).wait_recv()
+                total = total + self.chip_buf[r, c]
+            self.out[r, chip, core] = total
+            for c in others:
+                self.show(r, c, chip).start()
+            self.hand(r, chip, core).start()
+        for r in stages:
+            for c in others:
+                self.show(r, c, c).wait_recv()
+                self.hand(r, c, core).start()
+        for r in stages:
+            for c in plane.order:
+                self.hand(r, c, 1 - core).wait_recv()
+
+    def drain(self, stages):
+        for r in stages:
+            self.pair(r).wait_send()
+            for c in self.plane.order[1:]:
+                self.give(r, c).wait_send()
+                self.show(r, c, self.plane.chip).wait_send()
+            for c in self.plane.order:
+                self.hand(r, c, self.plane.core).wait_send()
 
 
 def eliminate(leaves):
@@ -342,14 +377,28 @@
         load_entries.wait()
         prepare_sketch(pattern_ref, contrib_buf, assembled_buf, columns_ref, targets_ref, held)
 
-    drain_gather = gather(omega_ref, gathered, sems[:6], prepare)
-    sketch(gathered[...].reshape(columns, window_rows), held, part)
-    drain_reduce = reduce(plane, part, window, pair_buf, sum_buf, chip_buf, sems[6:14])
+    stages = part.shape[0]
+    row_count, row_pos = lax.axis_size("row"), lax.axis_index("row")
+    summing = Reduce(plane, part, window, pair_buf, sum_buf, chip_buf, sems[6:14])
+    if stages == row_count:
+
+        def stage(block):
+            sketch(gathered[block].reshape(columns // stages, window_rows), held, part.at[block])
+            summing.begin(block)
+
+        drain_gather = gather(omega_ref, gathered, sems[:6], prepare, stage, summing.settle)
+        order = [lax.rem(row_pos + step, row_count) for step in range(row_count)]
+    else:
+        drain_gather = gather(omega_ref, gathered, sems[:6], prepare, lambda block: None, lambda block: None)
+        sketch(gathered[...].reshape(columns, window_rows), held, part.at[0])
+        summing.begin(0)
+        summing.settle(0)
+        order = [0]
+    summing.finish(order)
     drain_gather()
-    drain_reduce()
+    summing.drain(order)
 
     near_send, near_recv = sems[14:]
-    row_pos = lax.axis_index("row")
     near = {"row": row_pos + 1 - 2 * (row_pos % 2)}
 
     def send(leaf, block):
@@ -401,8 +450,10 @@
     own = omega.T.reshape(2, own_width // 2, window_rows)
     f32, bf16, dma = jnp.float32, jnp.bfloat16, pltpu.SemaphoreType.DMA
     any_space = pl.BlockSpec(memory_space=pl.ANY)
-    block = pltpu.VMEM((chips, width, window_rows), f32)
-    split_window = pltpu.VMEM((chips, 2, width, window_rows), f32)
+    stages = rows if columns // (rows * 2 * chips) >= SUB else 1
+    piece = width // stages
+    block = pltpu.VMEM((stages, chips, piece, window_rows), f32)
+    split_window = pltpu.VMEM((stages, chips, 2, piece, window_rows), f32)
     bases, coupling = pl.pallas_call(
         whole_kernel,
         out_shape=(
@@ -431,7 +482,8 @@
         ]
         + [dma((rows,))] * 5
         + [dma]
-        + [dma((chips,))] * 8
+        + [dma((stages,))] * 2
+        + [dma((stages, chips))] * 6
         + [dma((2, columns // NB))] * 2,
         compiler_params=pltpu.CompilerParams(
             collective_id=0, has_side_effects=True, vmem_limit_bytes=56 << 20

time: 65.4 us -> 59 us (0.902)
  Pallas kernels: 58.6 us -> 51.8 us
    pallas_call x1, Pallas kernels: 58.6 us -> 51.8 us  [local(): pl.pallas_call(whole_kernel, out_shape=(jax.ShapeDtypeStruct((width, wind...]
where the time goes in v3:
time: 59 us; the launch traced here: 58.3 us
  Pallas kernels  51.8 us (88%)
  local copies, waits for them, and re-layouts  3.89 us (7%)
  other arithmetic  1.34 us (2%)
  between operations  1.29 us (2%)
    pallas_call x1, Pallas kernels, local(): pl.pallas_call(whole_kernel, out_shape=(jax.ShapeDtypeStruct((width, wind...  51.8 us
    unnamed x2, local copies, waits for them, and re-layouts  3.04 us
    sub x1, other arithmetic, local(): lax.dynamic_slice_in_dim(child_maps, row_pos * tile_rows, tile_rows)  1.34 us

profile of v3, /device:TPU:0, one launch (start us, length us, event | category | flops | bytes accessed | tf_op | source)
XLA Modules:
  0.0 58.3 jit_solution(15564585158546148717)
XLA Ops:
  1.3 1.3 %subtract_bitcast_fusion = (s32[512,1]{0,1:T(1,128)S(1)}, s32[1,512]{1,0:T(1,128)}) fusion(s32[1,2048]{1,0:T(1,128)} %param.10, s32[]{:T(128)S(6)} %select_n.7, s32[]{:T(128)S(6)} %mul.15, s32[]{:T(128)S(6)} %mul.13, s32[]{:T(128)S(6)} %select_n.6), kind=kLoop, calls=%fused_computation | loop fusion | flops 1024 | bytes 8208 | tf_op jit(solution)/shard_map/sub | solution.py:449
  2.6 0.8 %copy.8.targets_ref = s32[512,1]{1,0:T(8,128)} copy(s32[512,1]{0,1:T(1,128)S(1)} %get-tuple-element.6) | data formatting | bytes 4096 | tf_op jit(solution)/shard_map/sub | solution.py:449
  3.5 51.8 %front_samples.1 = (f32[32,1024]{1,0:T(8,128)}, f32[1,2,32,256]{3,2,1,0:T(8,128)}) custom-call(s32[1]{0:T(128)S(6)} %copy.11.bound_ref, s32[4,4]{1,0:T(4,128)} %pattern_ref.1, f32[2,32,1024]{2,1,0:T(8,128)} %bitcast.6, f32[1,512,512]{2,1,0:T(8,128)} %contrib_ref.1, f32[1,512,1024]{2,1,0:T(8,128)} %assembled_ref.1, s32[1,512]{1,0:T(1,128)} %get-tuple-element.7.columns_ref, ...), custom_call_target="tpu_custom_call" | custom-call | tf_op jit(solution)/shard_map/front_samples/pallas_call | solution.py:457
  55.3 1.6 %copy.12 = f32[1024,32]{0,1:T(8,128)} copy(f32[1024,32]{0,1:T(8,128)} %bitcast.7) | data formatting | bytes 262144
  56.8 1.5 %copy.13 = f32[1,2,32,256]{3,2,1,0:T(8,128)} copy(f32[1,2,32,256]{3,2,1,0:T(8,128)} %get-tuple-element.11) | data formatting | bytes 131072

commit v4 on v3

--- a/solution.py
+++ b/solution.py
@@ -9,17 +9,12 @@
 NB = 64
 SUB = 8
 MESH = pl.DeviceIdType.MESH
-highest = lax.Precision.HIGHEST
 VMEM = pl.BlockSpec(memory_space=pltpu.VMEM)
 SMEM = pl.BlockSpec(memory_space=pltpu.SMEM)
 
 NN = (((1,), (0,)), ((), ()))
 NT = (((1,), (1,)), ((), ()))
 TN = (((0,), (0,)), ((), ()))
-
-
-def mm(a, b, dims=NN):
-    return lax.dot_general(a, b, dims, precision=highest, preferred_element_type=jnp.float32)
 
 
 def split(a):
@@ -78,7 +73,7 @@
     pl.semaphore_wait(barrier, plane.chips + jnp.minimum(me, 1) + jnp.minimum(count - 1 - me, 1))
 
 
-def gather(own_ref, out_ref, sems, prepare, stage, settle):
+def gather(own_ref, out_ref, sems, prepare, stage, settle, finalize):
     send_right, send_left, recv, swap_send, swap_recv, local_sem = sems
     count = lax.axis_size("row")
     me = lax.axis_index("row")
@@ -155,12 +150,21 @@
                 settle(me)
             if step > 2:
                 at_distance(step - 2, settle)
+            if step == 3:
+                finalize(me)
+            if step > 3:
+                at_distance(step - 3, finalize)
     at_distance(count - 1, staged)
     if count == 2:
         settle(me)
     if count > 2:
         at_distance(count - 2, settle)
+    if count < 4:
+        finalize(me)
+    for step in range(max(count - 3, 1), count - 1):
+        at_distance(step, finalize)
     at_distance(count - 1, settle)
+    at_distance(count - 1, finalize)
 
     def drain():
         for step in range(count):
@@ -178,18 +182,26 @@
         for step in range(1, count):
             swap(lax.rem(me + step, count)).wait_send()
 
-    return drain
-
-
-def prepare_sketch(pattern_ref, contrib, assembled, columns_ref, targets_ref, held):
+    def nearest(act):
+        act(me)
+        for step in range(1, count):
+            at_distance(step, act)
+
+    return drain, nearest
+
+
+def prepare_sketch(pattern_ref, contrib, assembled, maps_ref, held):
     pick, place, front, entries = held
     half = lax.axis_index("child")
     tile_rows, tile_cols = contrib.shape
     window_rows = assembled.shape[1]
-    lanes = lax.broadcasted_iota(jnp.int32, (window_rows, tile_cols), 0)
-    pick[...] = jnp.where(lanes == columns_ref[...], 1.0, 0.0).astype(jnp.bfloat16)
-    rows = lax.broadcasted_iota(jnp.int32, (tile_rows, window_rows), 1)
-    place[...] = jnp.where(rows == targets_ref[...], 1.0, 0.0).astype(jnp.bfloat16)
+    row_pos, col_pos = lax.axis_index("row"), lax.axis_index("col")
+    columns = maps_ref[:, pl.ds(pl.multiple_of(col_pos * tile_cols, tile_cols), tile_cols)] - col_pos * window_rows
+    targets = maps_ref[:, pl.ds(pl.multiple_of(row_pos * tile_rows, tile_rows), tile_rows)] - row_pos * window_rows
+    index = lax.broadcasted_iota(jnp.int32, (window_rows, tile_cols), 0)
+    pick[...] = jnp.where(index == columns, 1.0, 0.0).astype(jnp.bfloat16)
+    index = lax.broadcasted_iota(jnp.int32, (window_rows, tile_rows), 0)
+    place[...] = jnp.where(index == targets, 1.0, 0.0).astype(jnp.bfloat16)
     front[0], front[1] = split(contrib[...])
     for row in range(tile_rows // BT):
         for col in range(window_rows // BT):
@@ -207,12 +219,12 @@
 def sketch(omega, held, part_ref):
     pick, place, front, entries = held
     half = lax.axis_index("child")
-    rows, tile_rows = omega.shape[0], place.shape[0]
+    rows, tile_rows = omega.shape[0], place.shape[1]
     both = jnp.concatenate(split(omega), axis=0)
     picked = dot16(both, pick[...]).astype(jnp.bfloat16)
     product = stacked(picked, front, NT)
     sparse = stacked(both, entries, NT)
-    spread = dot16(jnp.concatenate(split(product), axis=0), place[...])
+    spread = dot16(jnp.concatenate(split(product), axis=0), place[...], NT)
     part_ref[...] = (spread[:rows] + spread[rows:]).reshape(part_ref.shape)
     where = pl.ds(pl.multiple_of(half * tile_rows, tile_rows), tile_rows)
     part_ref[:, :, :, where] = part_ref[:, :, :, where] + sparse.reshape(part_ref.shape[:3] + (tile_rows,))
@@ -258,25 +270,26 @@
             self.sum_buf[r, c] = self.part[r, c, plane.core] + self.pair_buf[r, c]
             self.give(r, c).start()
 
-    def finish(self, stages):
+    def finalize(self, r):
         plane = self.plane
         chip, core, others = plane.chip, plane.core, plane.order[1:]
-        for r in stages:
-            total = self.part[r, chip, core] + self.pair_buf[r, chip]
-            for c in others:
-                self.take(r, c).wait_recv()
-                total = total + self.chip_buf[r, c]
-            self.out[r, chip, core] = total
-            for c in others:
-                self.show(r, c, chip).start()
-            self.hand(r, chip, core).start()
-        for r in stages:
-            for c in others:
-                self.show(r, c, c).wait_recv()
-                self.hand(r, c, core).start()
-        for r in stages:
-            for c in plane.order:
-                self.hand(r, c, 1 - core).wait_recv()
+        total = self.part[r, chip, core] + self.pair_buf[r, chip]
+        for c in others:
+            self.take(r, c).wait_recv()
+            total = total + self.chip_buf[r, c]
+        self.out[r, chip, core] = total
+        for c in others:
+            self.show(r, c, chip).start()
+        self.hand(r, chip, core).start()
+
+    def forward(self, r):
+        for c in self.plane.order[1:]:
+            self.show(r, c, c).wait_recv()
+            self.hand(r, c, self.plane.core).start()
+
+    def arrive(self, r):
+        for c in self.plane.order:
+            self.hand(r, c, 1 - self.plane.core).wait_recv()
 
     def drain(self, stages):
         for r in stages:
@@ -350,7 +363,7 @@
         done = eliminate(aug)
         for leaf in range(2):
             inverse = jnp.concatenate(done[leaf], axis=0)[:, NB:]
-            rows = mm(inverse, work[leaf, begin:end, :])
+            rows = mm3(inverse, work[leaf, begin:end, :])
             work[leaf, begin:end, :] = rows
             done_block(leaf, block, begin, end, rows[:, :columns])
             if end < columns:
@@ -358,7 +371,7 @@
 
 
 def whole_kernel(
-    bound_ref, pattern_ref, omega_ref, contrib_ref, assembled_ref, columns_ref, targets_ref, bases_ref, coupling_ref,
+    bound_ref, pattern_ref, omega_ref, contrib_ref, assembled_ref, maps_ref, bases_ref, coupling_ref,
     gathered, contrib_buf, assembled_buf, pick, place, front, entries,
     part, window, pair_buf, sum_buf, chip_buf, work, upper, sibling, input_sems, *sems,
 ):
@@ -375,7 +388,7 @@
     def prepare():
         load_front.wait()
         load_entries.wait()
-        prepare_sketch(pattern_ref, contrib_buf, assembled_buf, columns_ref, targets_ref, held)
+        prepare_sketch(pattern_ref, contrib_buf, assembled_buf, maps_ref, held)
 
     stages = part.shape[0]
     row_count, row_pos = lax.axis_size("row"), lax.axis_index("row")
@@ -386,15 +399,22 @@
             sketch(gathered[block].reshape(columns // stages, window_rows), held, part.at[block])
             summing.begin(block)
 
-        drain_gather = gather(omega_ref, gathered, sems[:6], prepare, stage, summing.settle)
+        drain_gather, nearest = gather(
+            omega_ref, gathered, sems[:6], prepare, stage, summing.settle, summing.finalize
+        )
+        nearest(summing.forward)
         order = [lax.rem(row_pos + step, row_count) for step in range(row_count)]
     else:
-        drain_gather = gather(omega_ref, gathered, sems[:6], prepare, lambda block: None, lambda block: None)
+        idle = lambda block: None
+        drain_gather, nearest = gather(omega_ref, gathered, sems[:6], prepare, idle, idle, idle)
         sketch(gathered[...].reshape(columns, window_rows), held, part.at[0])
         summing.begin(0)
         summing.settle(0)
+        summing.finalize(0)
+        summing.forward(0)
         order = [0]
-    summing.finish(order)
+    for r in order:
+        summing.arrive(r)
     drain_gather()
     summing.drain(order)
 
@@ -435,6 +455,11 @@
             send(leaf, block).wait_send()
 
 
+def deliver_kernel(bases_ref, coupling_ref, bases_out, coupling_out):
+    bases_out[...] = bases_ref[...]
+    coupling_out[...] = coupling_ref[...]
+
+
 def local(contrib, assembled, pattern, omega, row_maps, leaf_bounds):
     tile_rows, tile_cols = contrib.shape[1:]
     window_rows, own_width = omega.shape
@@ -442,11 +467,6 @@
     chips = lax.axis_size("col") * lax.axis_size("child") // 2
     columns = own_width * rows
     width = columns // (2 * chips)
-    row_pos = lax.axis_index("row")
-    col_pos = lax.axis_index("col")
-    child_maps = row_maps[0]
-    col_maps = lax.dynamic_slice_in_dim(child_maps, col_pos * tile_cols, tile_cols) - col_pos * window_rows
-    targets = lax.dynamic_slice_in_dim(child_maps, row_pos * tile_rows, tile_rows) - row_pos * window_rows
     own = omega.T.reshape(2, own_width // 2, window_rows)
     f32, bf16, dma = jnp.float32, jnp.bfloat16, pltpu.SemaphoreType.DMA
     any_space = pl.BlockSpec(memory_space=pl.ANY)
@@ -460,14 +480,14 @@
             jax.ShapeDtypeStruct((width, window_rows), f32),
             jax.ShapeDtypeStruct((1, 2, width, columns), f32),
         ),
-        in_specs=[SMEM, SMEM, VMEM, any_space, any_space, VMEM, VMEM],
+        in_specs=[SMEM, SMEM, VMEM, any_space, any_space, VMEM],
         out_specs=(VMEM, VMEM),
         scratch_shapes=[
             pltpu.VMEM((rows, 2, own_width // 2, window_rows), f32),
             pltpu.VMEM((tile_rows, tile_cols), f32),
             pltpu.VMEM((tile_rows, window_rows), f32),
             pltpu.VMEM((window_rows, tile_cols), bf16),
-            pltpu.VMEM((tile_rows, window_rows), bf16),
+            pltpu.VMEM((window_rows, tile_rows), bf16),
             pltpu.VMEM((2, tile_rows, tile_cols), bf16),
             pltpu.VMEM((2, tile_rows, window_rows), bf16),
             split_window,
@@ -489,7 +509,17 @@
             collective_id=0, has_side_effects=True, vmem_limit_bytes=56 << 20
         ),
         name="front_samples",
-    )(leaf_bounds, pattern, own, contrib, assembled, col_maps[None, :], targets[:, None])
+    )(leaf_bounds, pattern, own, contrib, assembled, row_maps)
+    bases, coupling = pl.pallas_call(
+        deliver_kernel,
+        out_shape=(
+            jax.ShapeDtypeStruct(bases.shape, f32),
+            jax.ShapeDtypeStruct(coupling.shape, f32),
+        ),
+        in_specs=[VMEM, VMEM],
+        out_specs=(VMEM, VMEM),
+        name="deliver",
+    )(bases, coupling)
     return (bases.T, coupling)
 
 

time: 59 us -> 57.1 us (0.968)
  Pallas kernels: 51.8 us -> 55.7 us
  local copies, waits for them, and re-layouts: 3.89 us -> 0 us
  other arithmetic: 1.34 us -> 0 us
    unnamed x2 -> x0, local copies, waits for them, and re-layouts: 3.04 us -> none
    pallas_call x1, Pallas kernels: 51.8 us -> 54.1 us  [local(): pl.pallas_call(whole_kernel, out_shape=(jax.ShapeDtypeStruct((width, wind...]
    pallas_call x0 -> x1, Pallas kernels: none -> 1.59 us  [local(): pl.pallas_call(deliver_kernel, out_shape=(jax.ShapeDtypeStruct(bases.shap...]
    sub x1 -> x0, other arithmetic: 1.34 us -> none  [local(): lax.dynamic_slice_in_dim(child_maps, row_pos * tile_rows, tile_rows)]
    sub x1 -> x0, local copies, waits for them, and re-layouts: 0.84 us -> none  [local(): lax.dynamic_slice_in_dim(child_maps, row_pos * tile_rows, tile_rows)]
where the time goes in v4:
time: 57.1 us; the launch traced here: 56.9 us
  Pallas kernels  55.7 us (98%)
  between operations  1.29 us (2%)
    pallas_call x1, Pallas kernels, local(): pl.pallas_call(whole_kernel, out_shape=(jax.ShapeDtypeStruct((width, wind...  54.1 us
    pallas_call x1, Pallas kernels, local(): pl.pallas_call(deliver_kernel, out_shape=(jax.ShapeDtypeStruct(bases.shap...  1.59 us

profile of v4, /device:TPU:0, one launch (start us, length us, event | category | flops | bytes accessed | tf_op | source)
XLA Modules:
  0.0 56.9 jit_solution(14153804755208258567)
XLA Ops:
  1.3 54.1 %front_samples.1 = (f32[32,1024]{1,0:T(8,128)}, f32[1,2,32,256]{3,2,1,0:T(8,128)}) custom-call(s32[1]{0:T(128)S(6)} %copy.8.bound_ref, s32[4,4]{1,0:T(4,128)} %pattern_ref.1, f32[2,32,1024]{2,1,0:T(8,128)} %bitcast.4, f32[1,512,512]{2,1,0:T(8,128)} %contrib_ref.1, f32[1,512,1024]{2,1,0:T(8,128)} %assembled_ref.1, s32[1,2048]{1,0:T(1,128)} %maps_ref.1), custom_call_target="tpu_custom_call" | custom-call | tf_op jit(solution)/shard_map/front_samples/pallas_call | solution.py:477
  55.3 1.6 %deliver.1 = (f32[32,1024]{1,0:T(8,128)}, f32[1,2,32,256]{3,2,1,0:T(8,128)}) custom-call(f32[32,1024]{1,0:T(8,128)} %get-tuple-element.6.bases_ref, f32[1,2,32,256]{3,2,1,0:T(8,128)} %get-tuple-element.7.coupling_ref), custom_call_target="tpu_custom_call" | custom-call | tf_op jit(solution)/shard_map/deliver/pallas_call | solution.py:513

commit v5 on v4

--- a/solution.py
+++ b/solution.py
@@ -400,8 +400,9 @@
             summing.begin(block)
 
         drain_gather, nearest = gather(
-            omega_ref, gathered, sems[:6], prepare, stage, summing.settle, summing.finalize
+            omega_ref, gathered, sems[:6], prepare, stage, summing.settle, lambda block: None
         )
+        nearest(summing.finalize)
         nearest(summing.forward)
         order = [lax.rem(row_pos + step, row_count) for step in range(row_count)]
     else:

time: 57.1 us -> 54.6 us (0.956)
  Pallas kernels: 55.7 us -> 53.2 us
    pallas_call x1, Pallas kernels: 54.1 us -> 51.6 us  [local(): pl.pallas_call(whole_kernel, out_shape=(jax.ShapeDtypeStruct((width, wind...]
where the time goes in v5:
time: 54.6 us; the launch traced here: 54.4 us
  Pallas kernels  53.2 us (97%)
  between operations  1.29 us (2%)
    pallas_call x1, Pallas kernels, local(): pl.pallas_call(whole_kernel, out_shape=(jax.ShapeDtypeStruct((width, wind...  51.6 us
    pallas_call x1, Pallas kernels, local(): pl.pallas_call(deliver_kernel, out_shape=(jax.ShapeDtypeStruct(bases.shap...  1.59 us

profile of v5, /device:TPU:0, one launch (start us, length us, event | category | flops | bytes accessed | tf_op | source)
XLA Modules:
  0.0 54.4 jit_solution(2019589471476399)
XLA Ops:
  1.3 51.6 %front_samples.1 = (f32[32,1024]{1,0:T(8,128)}, f32[1,2,32,256]{3,2,1,0:T(8,128)}) custom-call(s32[1]{0:T(128)S(6)} %copy.8.bound_ref, s32[4,4]{1,0:T(4,128)} %pattern_ref.1, f32[2,32,1024]{2,1,0:T(8,128)} %bitcast.4, f32[1,512,512]{2,1,0:T(8,128)} %contrib_ref.1, f32[1,512,1024]{2,1,0:T(8,128)} %assembled_ref.1, s32[1,2048]{1,0:T(1,128)} %maps_ref.1), custom_call_target="tpu_custom_call" | custom-call | tf_op jit(solution)/shard_map/front_samples/pallas_call | solution.py:478
  52.9 1.6 %deliver.1 = (f32[32,1024]{1,0:T(8,128)}, f32[1,2,32,256]{3,2,1,0:T(8,128)}) custom-call(f32[32,1024]{1,0:T(8,128)} %get-tuple-element.6.bases_ref, f32[1,2,32,256]{3,2,1,0:T(8,128)} %get-tuple-element.7.coupling_ref), custom_call_target="tpu_custom_call" | custom-call | tf_op jit(solution)/shard_map/deliver/pallas_call | solution.py:514
